TPU v7x, 128 devices: a whole 4x4x4 slice. The times are simulated.
128 devices in a mesh: section: 2 (over core), dp: 16 (over y, x), mp: 4 (over z).
Axes of the slice: x: 4, y: 4, z: 4, core: 2. Of those that a mesh axis runs over, the one named last changes fastest.
Arguments:
- patches: bfloat16 [8192, 1280], P(('section', 'dp', 'mp')), may hold values from -6 to 6
- image_units: int32 [128, 3], P(('section', 'dp', 'mp')), may hold values from 1 to 8, 16 in all within a row
- v_gain: float32 [1280], replicated, may hold values from 0.5 to 1.5
- v_qkv: bfloat16 [1280, 3840], replicated, may hold values from -0.15625 to 0.15625
- v_out: bfloat16 [1280, 1280], replicated, may hold values from -0.15625 to 0.15625
- merge_gain: float32 [1280], replicated, may hold values from 0.5 to 1.5
- w_merge: bfloat16 [5120, 8192], P('dp', 'mp'), may hold values from -0.078125 to 0.078125
- routes: int32 [2048, 1], P(('section', 'dp', 'mp')), may hold values from 0 to 15; in each aligned block of 1024 rows (0 to 1023, 1024 to 2047, ...) at most 128 rows name the same one
- text: bfloat16 [4096, 8192], P(('section', 'dp'), 'mp'), may hold values from -6 to 6
- seq_lengths: int32 [32, 3], P(('section', 'dp')), may hold values from 1 to 64, 128 in all within a row
- lang_gain: float32 [2, 8192], P('section'), may hold values from 0.5 to 1.5
- w_qkv: bfloat16 [2, 8192, 5120], P('section', 'dp', 'mp'), may hold values from -0.0625 to 0.0625
- wo_t: bfloat16 [2, 8192, 4096], P('section', 'dp', 'mp'), may hold values from -0.09375 to 0.09375
- row_grads: bfloat16 [4096, 8192], P(('section', 'dp'), 'mp'), may hold values from -6 to 6
Outputs:
- final_hidden: bfloat16 [4096, 8192], P(('section', 'dp'), 'mp')
- merged_grads: bfloat16 [2048, 8192], P(('section', 'dp', 'mp'))
Inputs may be any that keep to these rules, and one draw needn't show every extreme that they name: `image_units`: each row sums to 16. `routes`: among the 1024 rows of one section index (aligned blocks), at most 128 name one group; in some section index one group is named by exactly 128. `seq_lengths`: each row sums to 128.
All inputs are finite; a program needn't handle non-finite values.
Results may differ from a plain program's by a relative error of at most 0.03.
Values may be sent and summed in bfloat16 or wider, within the bound.
A program may use at most 192 MiB of HBM per device.

v0:
```python
import math
import jax
import jax.numpy as jnp
from jax import lax
from jax.sharding import PartitionSpec as P

QH = 32
KVH = 4
HD = 128
VD = 1280
VH = 16
VHD = 80
MERGE = 4
EPSILON = 1e-06


def passed_along(value, axis, steps):
    count = lax.axis_size(axis)
    initial, last = (max(0, -steps), min(count, count - steps))
    return lax.ppermute(value, axis, [(source, source + steps) for source in range(initial, last)])


def broadcast(block, axis, owner):
    block = jnp.where(lax.axis_index(axis) == owner, block, jnp.zeros_like(block))
    return lax.psum(block, axis)


def layer_norm(values, norm_gain):
    values = values.astype(jnp.float32)
    centre = jnp.mean(values, axis=-1, keepdims=True)
    centred = values - centre
    variance = jnp.mean(centred * centred, axis=-1, keepdims=True)
    return centred * lax.rsqrt(variance + EPSILON) * norm_gain


def rms_norm(values, norm_gain):
    values = values.astype(jnp.float32)
    return (
        values * lax.rsqrt(jnp.mean(values * values, axis=-1, keepdims=True) + EPSILON) * norm_gain
    )


def segment_of(lengths, amount):
    boundary = jnp.cumsum(lengths.astype(jnp.int32))
    positions = jnp.arange(amount, dtype=jnp.int32)
    return jnp.sum((positions[:, None] >= boundary[None, :]).astype(jnp.int32), axis=1)


def vision_rows(patches, units, v_gain, v_qkv, v_out, merge_gain):
    amount = patches.shape[0]
    merged_count = amount // MERGE
    unit_image = segment_of(units, merged_count)
    image_ids = jnp.broadcast_to(unit_image[:, None], (merged_count, MERGE)).reshape(amount)
    v_normed = layer_norm(patches, v_gain).astype(jnp.bfloat16)
    projected = jnp.dot(v_normed, v_qkv, preferred_element_type=jnp.float32).astype(jnp.bfloat16)
    projected = projected.reshape(amount, 3, VH, VHD)
    scores = jnp.einsum(
        "qhd,khd->hqk", projected[:, 0], projected[:, 1], preferred_element_type=jnp.float32
    ) / math.sqrt(VHD)
    allowed = image_ids[:, None] == image_ids[None, :]
    scores = jnp.where(allowed[None], scores, -1e30)
    weights = jax.nn.softmax(scores, axis=-1).astype(jnp.bfloat16)
    attended = (
        jnp.einsum("hqk,khd->qhd", weights, projected[:, 2], preferred_element_type=jnp.float32)
        .astype(jnp.bfloat16)
        .reshape(amount, VD)
    )
    update = jnp.dot(attended, v_out, preferred_element_type=jnp.float32)
    v_hidden = (patches.astype(jnp.float32) + update).astype(jnp.bfloat16)
    merged = layer_norm(v_hidden, merge_gain).astype(jnp.bfloat16)
    return merged.reshape(merged_count, MERGE * VD)


def attend(projected, lengths):
    seq_rows = projected.shape[0]
    group_size = QH // KVH
    kv_here = projected.shape[1] // ((group_size + 2) * HD)
    heads_view = projected.reshape(seq_rows, kv_here, group_size + 2, HD)
    scores = jnp.einsum(
        "tkgd,skd->kgts",
        heads_view[:, :, :group_size],
        heads_view[:, :, group_size],
        preferred_element_type=jnp.float32,
    ) * (1.0 / math.sqrt(HD))
    seq_ids = segment_of(lengths, seq_rows)
    positions = jnp.arange(seq_rows, dtype=jnp.int32)
    allowed = (seq_ids[:, None] == seq_ids[None, :]) & (positions[:, None] >= positions[None, :])
    scores = jnp.where(allowed[None, None], scores, -1e30)
    weights = jax.nn.softmax(scores, axis=-1).astype(jnp.bfloat16)
    attended = jnp.einsum(
        "kgts,skd->tkgd",
        weights,
        heads_view[:, :, group_size + 1],
        preferred_element_type=jnp.float32,
    ).astype(jnp.bfloat16)
    return attended.reshape(seq_rows, kv_here * group_size * HD)


def shards(
    patches,
    image_units,
    v_gain,
    v_qkv,
    v_out,
    merge_gain,
    w_merge,
    routes,
    text,
    seq_lengths,
    lang_gain,
    w_qkv,
    wo_t,
    row_grads,
):
    merged = vision_rows(patches, image_units[0], v_gain, v_qkv, v_out, merge_gain)
    all_rows, all_routes = (
        lax.all_gather(merged, ("dp", "mp"), axis=0, tiled=True),
        lax.all_gather(routes, ("dp", "mp"), axis=0, tiled=True),
    )
    target = all_routes[:, 0]
    section_rows = target.shape[0]
    row_order = jnp.arange(section_rows, dtype=jnp.int32)
    matching = target[:, None] == target[None, :]
    position = jnp.sum(
        (matching & (row_order[:, None] > row_order[None, :])).astype(jnp.int32), axis=1
    )
    seq_rows = text.shape[0]
    slot_index = target * seq_rows + position
    group_here = lax.axis_index("dp")
    dp_count = lax.axis_size("dp")
    slice_width = w_merge.shape[0]
    row_slice = lax.dynamic_slice_in_dim(all_rows, group_here * slice_width, slice_width, 1)
    wanted = jnp.arange(seq_rows * lax.axis_size("dp"), dtype=jnp.int32)
    picker = (slot_index[None, :] == wanted[:, None]).astype(jnp.bfloat16)
    picked = jnp.dot(picker, row_slice, preferred_element_type=jnp.float32).astype(jnp.bfloat16)
    image_rows = lax.psum_scatter(
        jnp.dot(picked, w_merge, preferred_element_type=jnp.float32).astype(jnp.bfloat16),
        "dp",
        scatter_dimension=0,
        tiled=True,
    )
    present = jnp.sum((target == group_here).astype(jnp.int32))
    positions = jnp.arange(seq_rows, dtype=jnp.int32)
    entry_rows = jnp.where((positions < present)[:, None], image_rows, text)
    gathered = (
        lax.all_gather(w_qkv, "dp", axis=1, tiled=True),
        lax.all_gather(wo_t, "dp", axis=1, tiled=True),
    )
    qkv_weight = gathered[0][0]
    out_weight = gathered[1][0]
    norm_gain = lang_gain[0]
    sections = lax.axis_size("section")
    section_here = lax.axis_index("section")
    is_first = section_here == 0
    lengths_here = seq_lengths[0]
    entry_all, lengths_all = (
        lax.all_gather(entry_rows, "section", axis=0, tiled=True),
        lax.all_gather(seq_lengths, "section", axis=0, tiled=True),
    )
    carried = jnp.zeros_like(entry_rows)
    carried_lengths = lengths_here
    finished = []
    for section_step in range(2 * sections - 1):
        if section_step > 0:
            carried, carried_lengths = passed_along((carried, carried_lengths), "section", 1)
        if section_step < sections:
            incoming = entry_all[section_step * seq_rows : (section_step + 1) * seq_rows]
            incoming_lengths = lengths_all[section_step]
            carried = jnp.where(is_first, incoming, carried)
            carried_lengths = jnp.where(is_first, incoming_lengths, carried_lengths)
        features = lax.all_gather(carried, "mp", axis=1, tiled=True)
        normed = rms_norm(features, norm_gain).astype(jnp.bfloat16)
        projected = jnp.dot(normed, qkv_weight, preferred_element_type=jnp.float32)
        attended = attend(projected.astype(jnp.bfloat16), carried_lengths)
        partial_value = lax.dot_general(
            attended, out_weight, (((1,), (1,)), ((), ())), preferred_element_type=jnp.float32
        )
        update = lax.psum_scatter(
            partial_value.astype(jnp.bfloat16), "mp", scatter_dimension=1, tiled=True
        ).astype(jnp.float32)
        carried = (carried.astype(jnp.float32) + update).astype(jnp.bfloat16)
        if section_step >= sections - 1:
            finished.append(carried)
    returned_rows = broadcast(jnp.stack(finished), "section", sections - 1)
    final_hidden = lax.dynamic_index_in_dim(returned_rows, section_here, 0, keepdims=False)
    columns = row_grads.shape[1]
    picker = ((target == group_here)[:, None] & (position[:, None] == positions[None, :])).astype(
        jnp.bfloat16
    )
    outgoing = jnp.dot(picker, row_grads, preferred_element_type=jnp.float32).astype(jnp.bfloat16)
    outgoing = outgoing.reshape(dp_count, section_rows // dp_count, columns)
    returned = lax.all_to_all(
        lax.all_to_all(outgoing, "dp", split_axis=0, concat_axis=0, tiled=True),
        "mp",
        split_axis=1,
        concat_axis=2,
        tiled=True,
    )
    merged_grads = jnp.sum(returned.astype(jnp.float32), axis=0).astype(jnp.bfloat16)
    return (final_hidden, merged_grads)


def solution(mesh):
    in_specs = (
        P(("section", "dp", "mp"), None),
        P(("section", "dp", "mp"), None),
        P(),
        P(),
        P(),
        P(),
        P("dp", "mp"),
        P(("section", "dp", "mp"), None),
        P(("section", "dp"), "mp"),
        P(("section", "dp"), None),
        P("section", None),
        P("section", "dp", "mp"),
        P("section", "dp", "mp"),
        P(("section", "dp"), "mp"),
    )
    out_specs = (P(("section", "dp"), "mp"), P(("section", "dp", "mp"), None))
    return jax.shard_map(shards, mesh=mesh, in_specs=in_specs, out_specs=out_specs, check_vma=False)
```

profile of v0, /device:TPU:0, one launch (start us, length us, event | category | flops | bytes accessed | tf_op | source)
XLA Modules:
  0.0 799.6 jit_solution(8067572202809848577)
XLA Ops:
  9.6 6.6 convolution_convert_fusion.1
  16.2 3.1 reshape.446
  19.3 2.0 fusion.97
  21.8 1.3 fusion.60
  23.9 2.4 fusion.64
  26.3 1.8 copy.109
  28.1 1.9 reshape.449
  30.0 1.7 fusion.99
  34.4 24.9 %all-reduce = s32[1024]{0:T(1024)S(1)} all-reduce(s32[1024]{0:T(1024)S(1)} %bitcast_dynamic-update-slice_fusion), channel_id=1, replica_groups=mesh['section'=2,'dp'=16,'mp'=4] {'dp','mp'}, use_global_device_ids=true, to_apply=%add | all-reduce | flops 1024 | bytes 8192 | tf_op jit(solution)/shard_map/squeeze | solution.py:120
  60.4 60.5 %all-gather.9.cloned.1.call-done = bf16[1024,5120]{1,0:T(8,128)(2,1)} async-done(((bf16[16,5120]{1,0:T(8,128)(2,1)}), bf16[1024,5120]{1,0:T(8,128)(2,1)}) %all-gather.9.cloned.1.call-update) | async-done | bytes 10485776 | tf_op jit(solution)/shard_map/all_gather | solution.py:117
  120.9 10.7 %convolution_convert_fusion = bf16[2048,2048]{1,0:T(8,128)(2,1)} fusion(bf16[320,2048]{1,0:T(8,128)(2,1)} %param.20, s32[1024]{0:T(1024)S(1)} %get-tuple-element.7, bf16[1024,5120]{1,0:T(8,128)(2,1)} %all-gather.9.cloned.1.call-done, s32[]{:T(128)S(6)} %select_n.69), kind=kOutput, calls=%fused_computation.18 | convolution fusion | flops 4033478656 | bytes 10489860 | tf_op jit(solution)/shard_map/dot_general | solution.py:137
  132.4 83.8 %reduce-scatter.5.cloned.1.call-done = bf16[128,2048]{1,0:T(8,128)(2,1)} async-done(((bf16[2048,2048]{1,0:T(8,128)(2,1)}), bf16[128,2048]{1,0:T(8,128)(2,1)}) %reduce-scatter.5.cloned.1.call-update) | async-done | bytes 524304 | tf_op jit(solution)/shard_map/reduce_scatter | solution.py:136
  216.3 2.0 broadcast_select_fusion
  218.3 11.4 %all-gather.11.cloned.1.call-done = bf16[256,2048]{1,0:T(8,128)(2,1)} async-done(((bf16[128,2048]{1,0:T(8,128)(2,1)}), bf16[256,2048]{1,0:T(8,128)(2,1)}) %all-gather.11.cloned.1.call-update) | async-done | bytes 1048592 | tf_op jit(solution)/shard_map/all_gather | solution.py:157
  229.7 1.9 slice_select_fusion
  232.8 2.2 all-gather
  235.4 28.8 %all-gather.13.cloned.1.call-done = bf16[128,8192]{1,0:T(8,128)(2,1)} async-done(((bf16[128,2048]{1,0:T(8,128)(2,1)}), bf16[128,8192]{1,0:T(8,128)(2,1)}) %all-gather.13.cloned.1.call-update) | async-done | bytes 2097168 | tf_op jit(solution)/shard_map/all_gather | solution.py:171
  264.2 2.1 fusion.23
  266.3 132.4 %all-gather.15.cloned.1.call-done = bf16[1,8192,1280]{2,1,0:T(8,128)(2,1)} async-done(((bf16[1,512,1280]{2,1,0:T(8,128)(2,1)}), bf16[1,8192,1280]{2,1,0:T(8,128)(2,1)}) %all-gather.15.cloned.1.call-update) | async-done | bytes 20971536 | tf_op jit(solution)/shard_map/all_gather | solution.py:146
  398.7 10.6 %fusion.35 = bf16[128,1280]{1,0:T(8,128)(2,1)S(1)} fusion(bf16[1,8192,1280]{2,1,0:T(8,128)(2,1)} %all-gather.15.cloned.1.call-done, bf16[128,8192]{1,0:T(8,128)(2,1)} %all-gather.13.cloned.1.call-done, f32[8192]{0:T(1024)S(1)} %bitcast.203, f32[128]{0:T(128)S(1)} %add_rsqrt_fusion.2), kind=kOutput, calls=%fused_computation.41 | convolution fusion | flops 2688712704 | bytes 23429632 | tf_op jit(solution)/shard_map/dot_general | solution.py:173
  410.1 101.6 %all-gather.17.cloned.1.call-done = bf16[1,8192,1024]{2,1,0:T(8,128)(2,1)} async-done(((bf16[1,512,1024]{2,1,0:T(8,128)(2,1)}), bf16[1,8192,1024]{2,1,0:T(8,128)(2,1)}) %all-gather.17.cloned.1.call-update) | async-done | bytes 16777232 | tf_op jit(solution)/shard_map/all_gather | solution.py:147
  511.7 12.8 %fusion.13 = bf16[128,8192]{1,0:T(8,128)(2,1)} fusion(bf16[128,1024]{0,1:T(8,128)(2,1)S(1)} %bitcast.197, bf16[1,8192,1024]{2,1,0:T(8,128)(2,1)} %all-gather.17.cloned.1.call-done), kind=kOutput, calls=%fused_computation.13 | convolution fusion | flops 2148532224 | bytes 19136512 | tf_op jit(solution)/shard_map/dot_general | solution.py:175
  524.6 29.7 %reduce-scatter.7.cloned.1.call-done = bf16[128,2048]{1,0:T(8,128)(2,1)} async-done(((bf16[128,8192]{1,0:T(8,128)(2,1)}), bf16[128,2048]{1,0:T(8,128)(2,1)}) %reduce-scatter.7.cloned.1.call-update) | async-done | bytes 524304 | tf_op jit(solution)/shard_map/reduce_scatter | solution.py:178
  555.5 1.8 collective-permute-start
  557.3 1.5 collective-permute-done
  559.8 2.5 collective-permute-start.1
  563.2 27.3 %all-gather.19.cloned.1.call-done = bf16[128,8192]{1,0:T(8,128)(2,1)} async-done(((bf16[128,2048]{1,0:T(8,128)(2,1)}), bf16[128,8192]{1,0:T(8,128)(2,1)}) %all-gather.19.cloned.1.call-update) | async-done | bytes 2097168 | tf_op jit(solution)/shard_map/all_gather | solution.py:171
  590.5 2.1 fusion.26
  592.6 10.6 %fusion.38 = bf16[128,1280]{1,0:T(8,128)(2,1)S(1)} fusion(bf16[1,8192,1280]{2,1,0:T(8,128)(2,1)} %all-gather.15.cloned.1.call-done, bf16[128,8192]{1,0:T(8,128)(2,1)} %all-gather.19.cloned.1.call-done, f32[128]{0:T(128)S(1)} %add_rsqrt_fusion.1, f32[8192]{0:T(1024)S(1)} %bitcast.204), kind=kOutput, calls=%fused_computation.42 | convolution fusion | flops 2688712704 | bytes 23429632 | tf_op jit(solution)/shard_map/dot_general | solution.py:173
  604.0 12.8 %fusion.16 = bf16[128,8192]{1,0:T(8,128)(2,1)} fusion(bf16[128,1024]{0,1:T(8,128)(2,1)S(1)} %bitcast.199, bf16[1,8192,1024]{2,1,0:T(8,128)(2,1)} %all-gather.17.cloned.1.call-done), kind=kOutput, calls=%fused_computation.14 | convolution fusion | flops 2148532224 | bytes 19136512 | tf_op jit(solution)/shard_map/dot_general | solution.py:175
  616.9 29.9 %reduce-scatter.9.cloned.1.call-done = bf16[128,2048]{1,0:T(8,128)(2,1)} async-done(((bf16[128,8192]{1,0:T(8,128)(2,1)}), bf16[128,2048]{1,0:T(8,128)(2,1)}) %reduce-scatter.9.cloned.1.call-update) | async-done | bytes 524304 | tf_op jit(solution)/shard_map/reduce_scatter | solution.py:178
  648.0 1.8 collective-permute-start.2
  649.8 1.5 collective-permute-done.2
  652.1 3.1 convolution_convert_fusion.2
  655.2 6.9 all-to-all-start
  662.1 2.2 collective-permute-start.3
  665.3 17.6 %all-gather.21.cloned.1.call-done = bf16[128,8192]{1,0:T(8,128)(2,1)} async-done(((bf16[128,2048]{1,0:T(8,128)(2,1)}), bf16[128,8192]{1,0:T(8,128)(2,1)}) %all-gather.21.cloned.1.call-update) | async-done | bytes 2097168 | tf_op jit(solution)/shard_map/all_gather | solution.py:171
  682.9 2.1 fusion.29
  685.0 10.6 %fusion.41 = bf16[128,1280]{1,0:T(8,128)(2,1)S(1)} fusion(bf16[1,8192,1280]{2,1,0:T(8,128)(2,1)} %all-gather.15.cloned.1.call-done, bf16[128,8192]{1,0:T(8,128)(2,1)} %all-gather.21.cloned.1.call-done, f32[128]{0:T(128)S(1)} %add_rsqrt_fusion, f32[8192]{0:T(1024)S(1)} %bitcast.205), kind=kOutput, calls=%fused_computation.43 | convolution fusion | flops 2688712704 | bytes 23429632 | tf_op jit(solution)/shard_map/dot_general | solution.py:173
  696.5 12.8 %fusion.19 = bf16[128,8192]{1,0:T(8,128)(2,1)} fusion(bf16[128,1024]{0,1:T(8,128)(2,1)S(1)} %bitcast.198, bf16[1,8192,1024]{2,1,0:T(8,128)(2,1)} %all-gather.17.cloned.1.call-done), kind=kOutput, calls=%fused_computation.15 | convolution fusion | flops 2148532224 | bytes 19136512 | tf_op jit(solution)/shard_map/dot_general | solution.py:175
  709.3 16.7 %all-to-all-done = bf16[16,64,2048]{2,1,0:T(8,128)(2,1)} async-done(((bf16[16,64,2048]{2,1,0:T(8,128)(2,1)}), bf16[16,64,2048]{2,1,0:T(8,128)(2,1)}, u32[]{:S(2)}, u32[]{:S(2)}) %all-to-all-start) | async-done | bytes 4194336 | tf_op jit(solution)/shard_map/all_to_all | solution.py:193
  726.0 6.5 copy.122
  732.5 5.0 all-to-all-start.1
  737.5 1.7 reduce-scatter.11.cloned.1.call-done
  740.4 2.4 maximum_select_fusion
  742.8 43.2 %all-to-all-done.1 = bf16[16,64,2048]{2,0,1:T(8,128)(2,1)} async-done(((bf16[16,64,2048]{2,0,1:T(8,128)(2,1)}), bf16[16,64,2048]{2,0,1:T(8,128)(2,1)}, u32[]{:S(2)}, u32[]{:S(2)}) %all-to-all-start.1) | async-done | bytes 4194336 | tf_op jit(solution)/shard_map/all_to_all | solution.py:192
  786.0 3.9 reduce_sum.188
  790.7 1.9 dynamic-slice_bitcast_fusion
  (113 shorter events, 19.7 us)
Async XLA Ops:
  7.2 22.9 %copy-start = (bf16[1280,1280]{1,0:T(8,128)(2,1)S(1)}, bf16[1280,1280]{1,0:T(8,128)(2,1)}, u32[]{:S(2)}) copy-start(bf16[1280,1280]{1,0:T(8,128)(2,1)} %param.18) | copy-start | bytes 9830404
  7.2 113.7 %all-gather.9.cloned.1.call-start = ((), (), s32[]{:S(2)}) async-start(), calls=%async_computation.6 | async-start | bytes 10649600 | tf_op jit(solution)/shard_map/all_gather | solution.py:117
  9.6 11.7 %copy-start.13 = (s32[1,3]{1,0:T(1,128)S(1)}, s32[1,3]{1,0:T(1,128)}, u32[]{:S(2)}) copy-start(s32[1,3]{1,0:T(1,128)} %param.15) | copy-start | bytes 40
  16.2 13.9 %copy-start.3 = (bf16[64,1280]{1,0:T(8,128)(2,1)S(1)}, bf16[64,1280]{1,0:T(8,128)(2,1)}, u32[]{:S(2)}) copy-start(bf16[64,1280]{1,0:T(8,128)(2,1)} %param.14) | copy-start | bytes 491524
  23.1 0.8 copy-start.15
  23.1 8.9 %copy-start.10 = (f32[1280]{0:T(1024)S(1)}, f32[1280]{0:T(1024)}, u32[]{:S(2)}) copy-start(f32[1280]{0:T(1024)} %param.19) | copy-start | bytes 15364
  23.9 9.1 %copy-start.16 = (u32[128]{0:T(128)S(1)}, u32[128]{0:T(128)}, u32[]{:S(2)}) copy-start(u32[128]{0:T(128)} %constant.73) | copy-start | bytes 1540
  23.9 10.3 %copy-start.14 = (s32[16,1]{0,1:T(1,128)S(1)}, s32[16,1]{0,1:T(1,128)}, u32[]{:S(2)}) copy-start(s32[16,1]{0,1:T(1,128)} %param.21) | copy-start | bytes 196
  32.9 183.3 %reduce-scatter.5.cloned.1.call-start = ((), (), s32[]{:S(2)}) async-start(), calls=%async_computation.7 | async-start | bytes 8912896 | tf_op jit(solution)/shard_map/reduce_scatter | solution.py:136
  131.6 84.6 %copy-start.9 = (bf16[128,2048]{1,0:T(8,128)(2,1)S(1)}, bf16[128,2048]{1,0:T(8,128)(2,1)}, u32[]{:S(2)}) copy-start(bf16[128,2048]{1,0:T(8,128)(2,1)} %param.22) | copy-start | bytes 1572868
  131.7 101.1 %copy-start.11 = (s32[1,3]{1,0:T(1,128)S(1)}, s32[1,3]{1,0:T(1,128)}, u32[]{:S(2)}) copy-start(s32[1,3]{1,0:T(1,128)} %param.23) | copy-start | bytes 40
  131.7 267.0 %copy-start.12 = (f32[1,8192]{1,0:T(1,128)S(1)}, f32[1,8192]{1,0:T(1,128)}, u32[]{:S(2)}) copy-start(f32[1,8192]{1,0:T(1,128)} %param.24) | copy-start | bytes 98308
  131.7 98.0 %all-gather.11.cloned.1.call-start = ((), (), s32[]{:S(2)}) async-start(), calls=%async_computation.8 | async-start | bytes 1572864 | tf_op jit(solution)/shard_map/all_gather | solution.py:157
  218.2 46.0 %all-gather.13.cloned.1.call-start = ((), (), s32[]{:S(2)}) async-start(), calls=%async_computation.9 | async-start | bytes 2621440 | tf_op jit(solution)/shard_map/all_gather | solution.py:171
  231.6 167.1 %all-gather.15.cloned.1.call-start = ((), (), s32[]{:S(2)}) async-start(), calls=%async_computation.10 | async-start | bytes 22282240 | tf_op jit(solution)/shard_map/all_gather | solution.py:146
  232.2 279.5 %all-gather.17.cloned.1.call-start = ((), (), s32[]{:S(2)}) async-start(), calls=%async_computation.11 | async-start | bytes 17825792 | tf_op jit(solution)/shard_map/all_gather | solution.py:147
  232.7 321.6 %reduce-scatter.7.cloned.1.call-start = ((), (), s32[]{:S(2)}) async-start(), calls=%async_computation.12 | async-start | bytes 2621440 | tf_op jit(solution)/shard_map/reduce_scatter | solution.py:178
  511.7 42.6 %copy-start.4 = (bf16[256,2048]{1,0:T(8,128)(2,1)S(1)}, bf16[256,2048]{1,0:T(8,128)(2,1)}, u32[]{:S(2)}) copy-start(bf16[256,2048]{1,0:T(8,128)(2,1)} %all-gather.11.cloned.1.call-done) | copy-start | bytes 3145732
  524.5 66.0 %all-gather.19.cloned.1.call-start = ((), (), s32[]{:S(2)}) async-start(), calls=%async_computation.13 | async-start | bytes 2621440 | tf_op jit(solution)/shard_map/all_gather | solution.py:171
  555.5 3.3 collective-permute-start
  559.7 87.1 %reduce-scatter.9.cloned.1.call-start = ((), (), s32[]{:S(2)}) async-start(), calls=%async_computation.14 | async-start | bytes 2621440 | tf_op jit(solution)/shard_map/reduce_scatter | solution.py:178
  559.8 3.1 collective-permute-start.1
  604.0 42.7 %copy-start.2 = (bf16[128,2048]{1,0:T(8,128)(2,1)S(1)}, bf16[128,2048]{1,0:T(8,128)(2,1)}, u32[]{:S(2)}) copy-start(bf16[128,2048]{1,0:T(8,128)(2,1)} %slice_select_fusion.1) | copy-start | bytes 1572868
  616.8 35.3 %copy-start.8 = (bf16[128,2048]{1,0:T(8,128)(2,1)S(1)}, bf16[128,2048]{1,0:T(8,128)(2,1)}, u32[]{:S(2)}) copy-start(bf16[128,2048]{1,0:T(8,128)(2,1)} %param.27) | copy-start | bytes 1572868
  616.9 66.1 %all-gather.21.cloned.1.call-start = ((), (), s32[]{:S(2)}) async-start(), calls=%async_computation.15 | async-start | bytes 2621440 | tf_op jit(solution)/shard_map/all_gather | solution.py:171
  647.9 7.3 copy-start.5
  648.0 3.3 collective-permute-start.2
  651.3 0.8 copy-start.6
  655.2 70.8 %all-to-all-start = ((bf16[16,64,2048]{2,1,0:T(8,128)(2,1)}), bf16[16,64,2048]{2,1,0:T(8,128)(2,1)}, u32[]{:S(2)}, u32[]{:S(2)}) async-start(bf16[16,64,2048]{2,1,0:T(8,128)(2,1)} %bitcast.188), calls=%async_computation.4 | async-start | bytes 8388608 | tf_op jit(solution)/shard_map/all_to_all | solution.py:193
  662.1 77.1 %reduce-scatter.11.cloned.1.call-start = ((), (), s32[]{:S(2)}) async-start(), calls=%async_computation.16 | async-start | bytes 2621440 | tf_op jit(solution)/shard_map/reduce_scatter | solution.py:178
  662.1 2.8 collective-permute-start.3
  732.5 6.7 copy-start.7
  732.5 53.5 %all-to-all-start.1 = ((bf16[16,64,2048]{2,0,1:T(8,128)(2,1)}), bf16[16,64,2048]{2,0,1:T(8,128)(2,1)}, u32[]{:S(2)}, u32[]{:S(2)}) async-start(bf16[16,64,2048]{2,0,1:T(8,128)(2,1)} %copy.122), calls=%async_computation.5 | async-start | bytes 8388608 | tf_op jit(solution)/shard_map/all_to_all | solution.py:192
  737.5 53.2 %all-reduce.3.cloned.1.call-start = ((), (), s32[]{:S(2)}) async-start(), calls=%async_computation.17 | async-start | bytes 2097152 | tf_op jit(solution)/shard_map/psum | solution.py:25
  740.4 52.1 %copy-start.1 = (bf16[1280,1280]{1,0:T(8,128)(2,1)S(1)}, bf16[1280,1280]{1,0:T(8,128)(2,1)}, u32[]{:S(2)}) copy-start(bf16[1280,1280]{1,0:T(8,128)(2,1)} %param.18) | copy-start | bytes 9830404
Sparse Core Ops, SparseCore 0:
  33.0 87.8 all-gather.8
  131.8 84.4 reduce-scatter.4
  218.5 11.1 all-gather.10
  231.8 32.4 all-gather.12
  266.2 132.4 all-gather.14
  400.7 110.9 all-gather.16
  524.7 29.5 reduce-scatter.6
  559.8 30.6 all-gather.18
  617.0 29.7 reduce-scatter.8
  652.2 30.6 all-gather.20
  709.4 29.7 reduce-scatter.10
  742.9 26.6 all-reduce.2
where the time goes:
time: 808 us; the launch traced here: 800 us
  waiting for transfers between devices  590 us (73%)
  matrix products  97.5 us (12%)
  blocking collectives  27.2 us (3%)
  other arithmetic  27.1 us (3%)
  local copies, waits for them, and re-layouts  21.7 us (3%)
  starting transfers between devices  20.7 us (3%)
  between operations  15.5 us (2%)
    all_gather x1, waiting for transfers between devices, shards(): lax.all_gather(w_qkv, 'dp', axis=1, tiled=True)  132 us
    all_gather x1, waiting for transfers between devices, shards(): lax.all_gather(wo_t, 'dp', axis=1, tiled=True)  102 us
    reduce_scatter x1, waiting for transfers between devices, shards(): lax.psum_scatter(jnp.dot(picked, w_merge, preferred_element_type=jnp.floa...  83.8 us
    all_gather x3, waiting for transfers between devices, shards(): features = lax.all_gather(carried, 'mp', axis=1, tiled=True)  73.8 us
    reduce_scatter x3, waiting for transfers between devices, shards(): lax.psum_scatter(partial_value.astype(jnp.bfloat16), 'mp', scatter_dimens...  61.3 us
    all_gather x1, waiting for transfers between devices, shards(): lax.all_gather(merged, ('dp', 'mp'), axis=0, tiled=True)  60.5 us
    all_to_all x1, waiting for transfers between devices, shards(): lax.all_to_all(lax.all_to_all(outgoing, 'dp', split_axis=0, concat_axis=0...  43.2 us
    dot_general x3, matrix products, shards(): lax.dot_general(attended, out_weight, (((1,), (1,)), ((), ())), preferred...  38.4 us
  transfers between devices with their start and end apart: 18, of which 17 were waited for; matrix products, arithmetic and copies ran while one was open for 8% of the time, Pallas kernels for 0%

commit v1 on v0

--- a/solution.py
+++ b/solution.py
@@ -189,12 +189,20 @@
     )
     outgoing = jnp.dot(picker, row_grads, preferred_element_type=jnp.float32).astype(jnp.bfloat16)
     outgoing = outgoing.reshape(dp_count, section_rows // dp_count, columns)
-    returned = lax.all_to_all(
-        lax.all_to_all(outgoing, "dp", split_axis=0, concat_axis=0, tiled=True),
-        "mp",
-        split_axis=1,
-        concat_axis=2,
-        tiled=True,
+    returned = jnp.concatenate(
+        lax.all_to_all(
+            jnp.stack(
+                jnp.split(
+                    lax.all_to_all(outgoing, "dp", split_axis=0, concat_axis=0, tiled=True),
+                    lax.axis_size("mp"),
+                    axis=1,
+                )
+            ),
+            "mp",
+            0,
+            0,
+        ),
+        axis=2,
     )
     merged_grads = jnp.sum(returned.astype(jnp.float32), axis=0).astype(jnp.bfloat16)
     return (final_hidden, merged_grads)

time: 808 us -> 806 us (level)
  transfers between devices with their start and end apart: 18 -> 18, of which waited for: 17 -> 17; matrix products, arithmetic and copies ran while one was open for 8% -> 7% of each run, Pallas kernels for 0% -> 0%
where the time goes in v1:
time: 806 us; the launch traced here: 797 us
  waiting for transfers between devices  590 us (73%)
  matrix products  97.5 us (12%)
  other arithmetic  28.4 us (4%)
  blocking collectives  27.2 us (3%)
  starting transfers between devices  20.7 us (3%)
  local copies, waits for them, and re-layouts  18 us (2%)
  between operations  15.5 us (2%)
    all_gather x1, waiting for transfers between devices, shards(): lax.all_gather(w_qkv, 'dp', axis=1, tiled=True)  132 us
    all_gather x1, waiting for transfers between devices, shards(): lax.all_gather(wo_t, 'dp', axis=1, tiled=True)  102 us
    reduce_scatter x1, waiting for transfers between devices, shards(): lax.psum_scatter(jnp.dot(picked, w_merge, preferred_element_type=jnp.floa...  83.8 us
    all_gather x3, waiting for transfers between devices, shards(): features = lax.all_gather(carried, 'mp', axis=1, tiled=True)  73.8 us
    reduce_scatter x3, waiting for transfers between devices, shards(): lax.psum_scatter(partial_value.astype(jnp.bfloat16), 'mp', scatter_dimens...  62.6 us
    all_gather x1, waiting for transfers between devices, shards(): lax.all_gather(merged, ('dp', 'mp'), axis=0, tiled=True)  60.5 us
    all_to_all x1, waiting for transfers between devices, shards(): lax.all_to_all(jnp.stack(jnp.split(lax.all_to_all(outgoing, 'dp', split_a...  41.8 us
    dot_general x3, matrix products, shards(): lax.dot_general(attended, out_weight, (((1,), (1,)), ((), ())), preferred...  38.4 us
  transfers between devices with their start and end apart: 18, of which 17 were waited for; matrix products, arithmetic and copies ran while one was open for 7% of the time, Pallas kernels for 0%

profile of v1, /device:TPU:0, one launch (start us, length us, event | category | flops | bytes accessed | tf_op | source)
XLA Modules:
  0.0 797.3 jit_solution(16667692174789153264)
XLA Ops:
  9.6 6.6 convolution_convert_fusion.1
  16.2 3.1 reshape.447
  19.3 2.0 fusion.97
  23.9 2.4 fusion.64
  26.3 1.8 copy.88
  28.1 1.9 reshape.450
  30.0 1.7 fusion.99
  34.4 24.9 %all-reduce = s32[1024]{0:T(1024)S(1)} all-reduce(s32[1024]{0:T(1024)S(1)} %bitcast_dynamic-update-slice_fusion), channel_id=1, replica_groups=mesh['section'=2,'dp'=16,'mp'=4] {'dp','mp'}, use_global_device_ids=true, to_apply=%add | all-reduce | flops 1024 | bytes 8192 | tf_op jit(solution)/shard_map/squeeze | solution.py:120
  60.4 60.5 %all-gather.9.cloned.1.call-done = bf16[1024,5120]{1,0:T(8,128)(2,1)} async-done(((bf16[16,5120]{1,0:T(8,128)(2,1)}), bf16[1024,5120]{1,0:T(8,128)(2,1)}) %all-gather.9.cloned.1.call-update) | async-done | bytes 10485776 | tf_op jit(solution)/shard_map/all_gather | solution.py:117
  120.9 10.7 %convolution_convert_fusion = bf16[2048,2048]{1,0:T(8,128)(2,1)} fusion(bf16[320,2048]{1,0:T(8,128)(2,1)} %param.20, s32[1024]{0:T(1024)S(1)} %get-tuple-element.11, bf16[1024,5120]{1,0:T(8,128)(2,1)} %all-gather.9.cloned.1.call-done, s32[]{:T(128)S(6)} %select_n.69), kind=kOutput, calls=%fused_computation.18 | convolution fusion | flops 4033478656 | bytes 10489860 | tf_op jit(solution)/shard_map/dot_general | solution.py:137
  132.4 83.8 %reduce-scatter.5.cloned.1.call-done = bf16[128,2048]{1,0:T(8,128)(2,1)} async-done(((bf16[2048,2048]{1,0:T(8,128)(2,1)}), bf16[128,2048]{1,0:T(8,128)(2,1)}) %reduce-scatter.5.cloned.1.call-update) | async-done | bytes 524304 | tf_op jit(solution)/shard_map/reduce_scatter | solution.py:136
  216.3 2.0 broadcast_select_fusion
  218.3 11.4 %all-gather.11.cloned.1.call-done = bf16[256,2048]{1,0:T(8,128)(2,1)} async-done(((bf16[128,2048]{1,0:T(8,128)(2,1)}), bf16[256,2048]{1,0:T(8,128)(2,1)}) %all-gather.11.cloned.1.call-update) | async-done | bytes 1048592 | tf_op jit(solution)/shard_map/all_gather | solution.py:157
  229.7 1.9 slice_select_fusion
  232.8 2.2 all-gather
  235.4 28.8 %all-gather.13.cloned.1.call-done = bf16[128,8192]{1,0:T(8,128)(2,1)} async-done(((bf16[128,2048]{1,0:T(8,128)(2,1)}), bf16[128,8192]{1,0:T(8,128)(2,1)}) %all-gather.13.cloned.1.call-update) | async-done | bytes 2097168 | tf_op jit(solution)/shard_map/all_gather | solution.py:171
  264.2 2.1 fusion.23
  266.3 132.4 %all-gather.15.cloned.1.call-done = bf16[1,8192,1280]{2,1,0:T(8,128)(2,1)} async-done(((bf16[1,512,1280]{2,1,0:T(8,128)(2,1)}), bf16[1,8192,1280]{2,1,0:T(8,128)(2,1)}) %all-gather.15.cloned.1.call-update) | async-done | bytes 20971536 | tf_op jit(solution)/shard_map/all_gather | solution.py:146
  398.7 10.6 %fusion.35 = bf16[128,1280]{1,0:T(8,128)(2,1)S(1)} fusion(bf16[1,8192,1280]{2,1,0:T(8,128)(2,1)} %all-gather.15.cloned.1.call-done, bf16[128,8192]{1,0:T(8,128)(2,1)} %all-gather.13.cloned.1.call-done, f32[8192]{0:T(1024)S(1)} %bitcast.209, f32[128]{0:T(128)S(1)} %add_rsqrt_fusion.2), kind=kOutput, calls=%fused_computation.42 | convolution fusion | flops 2688712704 | bytes 23429632 | tf_op jit(solution)/shard_map/dot_general | solution.py:173
  410.1 101.6 %all-gather.17.cloned.1.call-done = bf16[1,8192,1024]{2,1,0:T(8,128)(2,1)} async-done(((bf16[1,512,1024]{2,1,0:T(8,128)(2,1)}), bf16[1,8192,1024]{2,1,0:T(8,128)(2,1)}) %all-gather.17.cloned.1.call-update) | async-done | bytes 16777232 | tf_op jit(solution)/shard_map/all_gather | solution.py:147
  511.7 12.8 %fusion.13 = bf16[128,8192]{1,0:T(8,128)(2,1)} fusion(bf16[128,1024]{0,1:T(8,128)(2,1)S(1)} %bitcast.203, bf16[1,8192,1024]{2,1,0:T(8,128)(2,1)} %all-gather.17.cloned.1.call-done), kind=kOutput, calls=%fused_computation.13 | convolution fusion | flops 2148532224 | bytes 19136512 | tf_op jit(solution)/shard_map/dot_general | solution.py:175
  524.6 29.7 %reduce-scatter.7.cloned.1.call-done = bf16[128,2048]{1,0:T(8,128)(2,1)} async-done(((bf16[128,8192]{1,0:T(8,128)(2,1)}), bf16[128,2048]{1,0:T(8,128)(2,1)}) %reduce-scatter.7.cloned.1.call-update) | async-done | bytes 524304 | tf_op jit(solution)/shard_map/reduce_scatter | solution.py:178
  555.5 1.8 collective-permute-start
  557.3 1.5 collective-permute-done
  559.8 2.5 collective-permute-start.1
  563.2 27.3 %all-gather.19.cloned.1.call-done = bf16[128,8192]{1,0:T(8,128)(2,1)} async-done(((bf16[128,2048]{1,0:T(8,128)(2,1)}), bf16[128,8192]{1,0:T(8,128)(2,1)}) %all-gather.19.cloned.1.call-update) | async-done | bytes 2097168 | tf_op jit(solution)/shard_map/all_gather | solution.py:171
  590.5 2.1 fusion.26
  592.6 10.6 %fusion.38 = bf16[128,1280]{1,0:T(8,128)(2,1)S(1)} fusion(bf16[1,8192,1280]{2,1,0:T(8,128)(2,1)} %all-gather.15.cloned.1.call-done, bf16[128,8192]{1,0:T(8,128)(2,1)} %all-gather.19.cloned.1.call-done, f32[128]{0:T(128)S(1)} %add_rsqrt_fusion.1, f32[8192]{0:T(1024)S(1)} %bitcast.210), kind=kOutput, calls=%fused_computation.43 | convolution fusion | flops 2688712704 | bytes 23429632 | tf_op jit(solution)/shard_map/dot_general | solution.py:173
  604.0 12.8 %fusion.16 = bf16[128,8192]{1,0:T(8,128)(2,1)} fusion(bf16[128,1024]{0,1:T(8,128)(2,1)S(1)} %bitcast.205, bf16[1,8192,1024]{2,1,0:T(8,128)(2,1)} %all-gather.17.cloned.1.call-done), kind=kOutput, calls=%fused_computation.14 | convolution fusion | flops 2148532224 | bytes 19136512 | tf_op jit(solution)/shard_map/dot_general | solution.py:175
  616.9 29.9 %reduce-scatter.9.cloned.1.call-done = bf16[128,2048]{1,0:T(8,128)(2,1)} async-done(((bf16[128,8192]{1,0:T(8,128)(2,1)}), bf16[128,2048]{1,0:T(8,128)(2,1)}) %reduce-scatter.9.cloned.1.call-update) | async-done | bytes 524304 | tf_op jit(solution)/shard_map/reduce_scatter | solution.py:178
  648.0 1.8 collective-permute-start.2
  649.8 1.5 collective-permute-done.2
  652.1 3.1 convolution_convert_fusion.2
  655.2 6.9 all-to-all-start
  662.1 2.2 collective-permute-start.3
  665.3 17.6 %all-gather.21.cloned.1.call-done = bf16[128,8192]{1,0:T(8,128)(2,1)} async-done(((bf16[128,2048]{1,0:T(8,128)(2,1)}), bf16[128,8192]{1,0:T(8,128)(2,1)}) %all-gather.21.cloned.1.call-update) | async-done | bytes 2097168 | tf_op jit(solution)/shard_map/all_gather | solution.py:171
  682.9 2.1 fusion.29
  685.0 10.6 %fusion.41 = bf16[128,1280]{1,0:T(8,128)(2,1)S(1)} fusion(bf16[1,8192,1280]{2,1,0:T(8,128)(2,1)} %all-gather.15.cloned.1.call-done, bf16[128,8192]{1,0:T(8,128)(2,1)} %all-gather.21.cloned.1.call-done, f32[128]{0:T(128)S(1)} %add_rsqrt_fusion, f32[8192]{0:T(1024)S(1)} %bitcast.211), kind=kOutput, calls=%fused_computation.44 | convolution fusion | flops 2688712704 | bytes 23429632 | tf_op jit(solution)/shard_map/dot_general | solution.py:173
  696.5 12.8 %fusion.19 = bf16[128,8192]{1,0:T(8,128)(2,1)} fusion(bf16[128,1024]{0,1:T(8,128)(2,1)S(1)} %bitcast.204, bf16[1,8192,1024]{2,1,0:T(8,128)(2,1)} %all-gather.17.cloned.1.call-done), kind=kOutput, calls=%fused_computation.15 | convolution fusion | flops 2148532224 | bytes 19136512 | tf_op jit(solution)/shard_map/dot_general | solution.py:175
  709.3 16.7 %all-to-all-done = bf16[16,64,2048]{2,1,0:T(8,128)(2,1)} async-done(((bf16[16,64,2048]{2,1,0:T(8,128)(2,1)}), bf16[16,64,2048]{2,1,0:T(8,128)(2,1)}, u32[]{:S(2)}, u32[]{:S(2)}) %all-to-all-start) | async-done | bytes 4194336 | tf_op jit(solution)/shard_map/all_to_all | solution.py:196
  726.0 2.8 slice_bitcast_fusion.3
  728.8 2.3 pad_maximum_fusion
  731.1 5.0 all-to-all-start.1
  736.2 3.1 reduce-scatter.11.cloned.1.call-done
  740.4 2.4 maximum_select_fusion
  742.8 41.8 %all-to-all-done.1 = bf16[4,16,16,2048]{3,2,1,0:T(8,128)(2,1)} async-done(((bf16[4,16,16,2048]{3,2,1,0:T(8,128)(2,1)}), bf16[4,16,16,2048]{3,2,1,0:T(8,128)(2,1)}, u32[]{:S(2)}, u32[]{:S(2)}) %all-to-all-start.1) | async-done | bytes 4194336 | tf_op jit(solution)/shard_map/all_to_all | solution.py:193
  784.7 2.9 reduce_sum.186
  788.3 1.9 dynamic-slice_bitcast_fusion
  (114 shorter events, 21.0 us)
Async XLA Ops:
  7.2 22.9 %copy-start = (bf16[1280,1280]{1,0:T(8,128)(2,1)S(1)}, bf16[1280,1280]{1,0:T(8,128)(2,1)}, u32[]{:S(2)}) copy-start(bf16[1280,1280]{1,0:T(8,128)(2,1)} %param.18) | copy-start | bytes 9830404
  7.2 113.7 %all-gather.9.cloned.1.call-start = ((), (), s32[]{:S(2)}) async-start(), calls=%async_computation.6 | async-start | bytes 10649600 | tf_op jit(solution)/shard_map/all_gather | solution.py:117
  9.6 11.7 %copy-start.13 = (s32[1,3]{1,0:T(1,128)S(1)}, s32[1,3]{1,0:T(1,128)}, u32[]{:S(2)}) copy-start(s32[1,3]{1,0:T(1,128)} %param.15) | copy-start | bytes 40
  16.2 13.9 %copy-start.3 = (bf16[64,1280]{1,0:T(8,128)(2,1)S(1)}, bf16[64,1280]{1,0:T(8,128)(2,1)}, u32[]{:S(2)}) copy-start(bf16[64,1280]{1,0:T(8,128)(2,1)} %param.14) | copy-start | bytes 491524
  23.1 0.8 copy-start.15
  23.1 8.9 %copy-start.10 = (f32[1280]{0:T(1024)S(1)}, f32[1280]{0:T(1024)}, u32[]{:S(2)}) copy-start(f32[1280]{0:T(1024)} %param.19) | copy-start | bytes 15364
  23.9 9.1 %copy-start.16 = (u32[128]{0:T(128)S(1)}, u32[128]{0:T(128)}, u32[]{:S(2)}) copy-start(u32[128]{0:T(128)} %constant.73) | copy-start | bytes 1540
  23.9 10.3 %copy-start.14 = (s32[16,1]{0,1:T(1,128)S(1)}, s32[16,1]{0,1:T(1,128)}, u32[]{:S(2)}) copy-start(s32[16,1]{0,1:T(1,128)} %param.21) | copy-start | bytes 196
  32.9 183.3 %reduce-scatter.5.cloned.1.call-start = ((), (), s32[]{:S(2)}) async-start(), calls=%async_computation.7 | async-start | bytes 8912896 | tf_op jit(solution)/shard_map/reduce_scatter | solution.py:136
  131.6 84.6 %copy-start.9 = (bf16[128,2048]{1,0:T(8,128)(2,1)S(1)}, bf16[128,2048]{1,0:T(8,128)(2,1)}, u32[]{:S(2)}) copy-start(bf16[128,2048]{1,0:T(8,128)(2,1)} %param.22) | copy-start | bytes 1572868
  131.7 101.1 %copy-start.11 = (s32[1,3]{1,0:T(1,128)S(1)}, s32[1,3]{1,0:T(1,128)}, u32[]{:S(2)}) copy-start(s32[1,3]{1,0:T(1,128)} %param.23) | copy-start | bytes 40
  131.7 267.0 %copy-start.12 = (f32[1,8192]{1,0:T(1,128)S(1)}, f32[1,8192]{1,0:T(1,128)}, u32[]{:S(2)}) copy-start(f32[1,8192]{1,0:T(1,128)} %param.24) | copy-start | bytes 98308
  131.7 98.0 %all-gather.11.cloned.1.call-start = ((), (), s32[]{:S(2)}) async-start(), calls=%async_computation.8 | async-start | bytes 1572864 | tf_op jit(solution)/shard_map/all_gather | solution.py:157
  218.2 46.0 %all-gather.13.cloned.1.call-start = ((), (), s32[]{:S(2)}) async-start(), calls=%async_computation.9 | async-start | bytes 2621440 | tf_op jit(solution)/shard_map/all_gather | solution.py:171
  231.6 167.1 %all-gather.15.cloned.1.call-start = ((), (), s32[]{:S(2)}) async-start(), calls=%async_computation.10 | async-start | bytes 22282240 | tf_op jit(solution)/shard_map/all_gather | solution.py:146
  232.2 279.5 %all-gather.17.cloned.1.call-start = ((), (), s32[]{:S(2)}) async-start(), calls=%async_computation.11 | async-start | bytes 17825792 | tf_op jit(solution)/shard_map/all_gather | solution.py:147
  232.7 321.6 %reduce-scatter.7.cloned.1.call-start = ((), (), s32[]{:S(2)}) async-start(), calls=%async_computation.12 | async-start | bytes 2621440 | tf_op jit(solution)/shard_map/reduce_scatter | solution.py:178
  511.7 42.6 %copy-start.4 = (bf16[256,2048]{1,0:T(8,128)(2,1)S(1)}, bf16[256,2048]{1,0:T(8,128)(2,1)}, u32[]{:S(2)}) copy-start(bf16[256,2048]{1,0:T(8,128)(2,1)} %all-gather.11.cloned.1.call-done) | copy-start | bytes 3145732
  524.5 66.0 %all-gather.19.cloned.1.call-start = ((), (), s32[]{:S(2)}) async-start(), calls=%async_computation.13 | async-start | bytes 2621440 | tf_op jit(solution)/shard_map/all_gather | solution.py:171
  555.5 3.3 collective-permute-start
  559.7 87.1 %reduce-scatter.9.cloned.1.call-start = ((), (), s32[]{:S(2)}) async-start(), calls=%async_computation.14 | async-start | bytes 2621440 | tf_op jit(solution)/shard_map/reduce_scatter | solution.py:178
  559.8 3.1 collective-permute-start.1
  604.0 42.7 %copy-start.2 = (bf16[128,2048]{1,0:T(8,128)(2,1)S(1)}, bf16[128,2048]{1,0:T(8,128)(2,1)}, u32[]{:S(2)}) copy-start(bf16[128,2048]{1,0:T(8,128)(2,1)} %slice_select_fusion.1) | copy-start | bytes 1572868
  616.8 35.3 %copy-start.8 = (bf16[128,2048]{1,0:T(8,128)(2,1)S(1)}, bf16[128,2048]{1,0:T(8,128)(2,1)}, u32[]{:S(2)}) copy-start(bf16[128,2048]{1,0:T(8,128)(2,1)} %param.27) | copy-start | bytes 1572868
  616.9 66.1 %all-gather.21.cloned.1.call-start = ((), (), s32[]{:S(2)}) async-start(), calls=%async_computation.15 | async-start | bytes 2621440 | tf_op jit(solution)/shard_map/all_gather | solution.py:171
  647.9 7.3 copy-start.5
  648.0 3.3 collective-permute-start.2
  651.3 0.8 copy-start.6
  655.2 70.8 %all-to-all-start = ((bf16[16,64,2048]{2,1,0:T(8,128)(2,1)}), bf16[16,64,2048]{2,1,0:T(8,128)(2,1)}, u32[]{:S(2)}, u32[]{:S(2)}) async-start(bf16[16,64,2048]{2,1,0:T(8,128)(2,1)} %bitcast.194), calls=%async_computation.4 | async-start | bytes 8388608 | tf_op jit(solution)/shard_map/all_to_all | solution.py:196
  662.1 77.1 %reduce-scatter.11.cloned.1.call-start = ((), (), s32[]{:S(2)}) async-start(), calls=%async_computation.16 | async-start | bytes 2621440 | tf_op jit(solution)/shard_map/reduce_scatter | solution.py:178
  662.1 2.8 collective-permute-start.3
  731.1 8.1 %copy-start.7 = (bf16[128,2048]{1,0:T(8,128)(2,1)S(1)}, bf16[128,2048]{1,0:T(8,128)(2,1)}, u32[]{:S(2)}) copy-start(bf16[128,2048]{1,0:T(8,128)(2,1)} %copy-done.6) | copy-start | bytes 1572868
  731.1 53.5 %all-to-all-start.1 = ((bf16[4,16,16,2048]{3,2,1,0:T(8,128)(2,1)}), bf16[4,16,16,2048]{3,2,1,0:T(8,128)(2,1)}, u32[]{:S(2)}, u32[]{:S(2)}) async-start(bf16[4,16,16,2048]{3,2,1,0:T(8,128)(2,1)} %pad_maximum_fusion), calls=%async_computation.5 | async-start | bytes 8388608 | tf_op jit(solution)/shard_map/all_to_all | solution.py:193
  736.1 52.2 %all-reduce.3.cloned.1.call-start = ((), (), s32[]{:S(2)}) async-start(), calls=%async_computation.17 | async-start | bytes 2097152 | tf_op jit(solution)/shard_map/psum | solution.py:25
  740.4 49.8 %copy-start.1 = (bf16[1280,1280]{1,0:T(8,128)(2,1)S(1)}, bf16[1280,1280]{1,0:T(8,128)(2,1)}, u32[]{:S(2)}) copy-start(bf16[1280,1280]{1,0:T(8,128)(2,1)} %param.18) | copy-start | bytes 9830404
Sparse Core Ops, SparseCore 0:
  33.0 87.8 all-gather.8
  131.8 84.4 reduce-scatter.4
  218.5 11.1 all-gather.10
  231.8 32.4 all-gather.12
  266.2 132.4 all-gather.14
  400.7 110.9 all-gather.16
  524.7 29.5 reduce-scatter.6
  559.8 30.6 all-gather.18
  617.0 29.7 reduce-scatter.8
  652.2 30.6 all-gather.20
  709.4 29.7 reduce-scatter.10
  742.9 28.0 all-reduce.2
